TPU v7x, 256 devices: a whole 4x4x8 slice. The times are simulated.
256 devices in a mesh: section: 8 (over y, z_hi), dp: 16 (over z_lo, x), tensor: 2 (over core).
Axes of the slice: x: 4, y: 4, z: 8 (z_hi: 2, z_lo: 4; z = z_hi * 4 + z_lo), core: 2. Of those that a mesh axis runs over, the one named last changes fastest.
Arguments:
- fwd_input: bfloat16 [8, 512, 2048], P('section', 'dp'), may hold values from -40 to 40
- fresh_input: bfloat16 [512, 2048], P('dp'), may hold values from -40 to 40
- cotangent: bfloat16 [8, 512, 2048], P('section', 'dp'), may hold values from -40 to 40
- fresh_cotangent: bfloat16 [512, 2048], P('dp'), may hold values from -40 to 40
- stash: bfloat16 [8, 2, 512, 2048], P('section', None, 'dp'), may hold values from -40 to 40
- norm_gain: float32 [8, 2048], P('section'), may hold values from 0.25 to 1.75
- qk_gain: float32 [8, 2, 128], P('section'), may hold values from 0.25 to 1.75
- w_query: bfloat16 [8, 2048, 2048], P('section', 'dp', 'tensor'), may hold values from -0.125 to 0.125
- w_key: bfloat16 [8, 2048, 256], P('section', 'dp', 'tensor'), may hold values from -0.125 to 0.125
- w_value: bfloat16 [8, 2048, 256], P('section', 'dp', 'tensor'), may hold values from -0.125 to 0.125
- w_out: bfloat16 [8, 2048, 2048], P('section', 'dp', 'tensor'), may hold values from -0.125 to 0.125
Outputs:
- out_activations: bfloat16 [8, 2, 512, 2048], P('section', None, 'dp')
- grad_input: bfloat16 [8, 2, 512, 2048], P('section', None, 'dp')
- grad_query: float32 [8, 2048, 2048], P('section', 'dp', 'tensor')
- grad_key: float32 [8, 2048, 256], P('section', 'dp', 'tensor')
- grad_value: float32 [8, 2048, 256], P('section', 'dp', 'tensor')
- grad_out: float32 [8, 2048, 2048], P('section', 'dp', 'tensor')
- grad_norm_gain: float32 [8, 2048], P('section')
- grad_qk_gain: float32 [8, 2, 128], P('section')
All inputs are finite; a program needn't handle non-finite values.
Results may differ from a plain program's by a relative error of at most 0.02.
Values may be sent and summed in bfloat16 or wider, within the bound.
No kernel may reach another device: no remote copies, remote signals or barrier semaphores. Data moves between devices by JAX's collectives and lax.ppermute only.
A program may use at most 64 MiB of HBM per device.

v0:
```python
import functools
import math

import jax
import jax.numpy as jnp
from jax import lax
from jax.experimental import pallas as pl
from jax.experimental.pallas import tpu as pltpu
from jax.sharding import PartitionSpec as P


HD = 128
EPSILON = 1e-06
THETA = 1000000.0
SIDE = 4
F32 = jnp.float32
BF16 = jnp.bfloat16
INTERPRET = False
Z_AT, X_AT, CORE_AT = 4, 5, 6
VMEM_LIMIT = 16 * 1024 * 1024


LINE_RING = {0: 1, 1: 3, 3: 2, 2: 0}


def z_ring():
    return [(z * SIDE + x, LINE_RING[z] * SIDE + x) for z in range(SIDE) for x in range(SIDE)]


def z_flip(k):
    return [(z * SIDE + x, (z ^ k) * SIDE + x) for z in range(SIDE) for x in range(SIDE)]


def x_flip(k):
    return [(z * SIDE + x, z * SIDE + (x ^ k)) for z in range(SIDE) for x in range(SIDE)]


def along_dp(array, route):
    return lax.ppermute(array, "dp", route)


def other_core(array):
    return lax.ppermute(array, "tensor", [(0, 1), (1, 0)])


def held_until(array, other):
    corner = other[(0,) * (other.ndim - 2)][:16, :HD]
    return lax.optimization_barrier((array, corner))[0]


def gather_weights(shard, z):
    rows = shard.shape[0]
    half = rows // 2
    held = [shard]
    for _ in range(1, SIDE):
        held.append(along_dp(held[-1], z_ring()))
    pieces, sources = [], []
    source = z
    for step, mine in enumerate(held):
        near = along_dp(mine, x_flip(1))
        wrap = along_dp(mine, x_flip(3))
        if step < 2:
            far_top = near[:half]
            far_low = wrap[half:]
            far_top = along_dp(far_top, x_flip(3))
            far_low = along_dp(far_low, x_flip(1))
            across = far_top, far_low
            if step == 1:
                across = (jnp.concatenate(across, axis=0),)
        else:
            across = (along_dp(across[0], z_ring()),)
        pieces.append((mine, near, wrap, *across))
        sources.append(source)
        source = jnp.where(source == 0, 2, jnp.where(source == 1, 0, jnp.where(source == 2, 3, 1)))
    return pieces, jnp.stack(sources)


FLIPS = [(j, k) for j in (0, 1, 3, 2) for k in range(SIDE)]


def gather_rows(block, gate):
    flips = [along_dp(block, z_flip(k)) for k in range(1, SIDE)]
    flips = [held_until(flip, gate) for flip in flips]
    mine = jnp.concatenate([block] + flips, axis=0)
    return mine, *spread_along_x(mine, mine)


def spread_along_x(to_near, to_wrap):
    half = to_near.shape[0] // 2
    near = along_dp(to_near, x_flip(1))
    wrap = along_dp(to_wrap, x_flip(3))
    far_top = along_dp(near[:half], x_flip(3))
    far_low = along_dp(wrap[half:], x_flip(1))
    return near, wrap, far_top, far_low


def sent_along_x(parted):
    flips = [along_dp(parted[j], x_flip(j)) for j in range(1, SIDE)]
    return parted[:1] + flips


def own_features(came):
    width = came[0].shape[1] // SIDE
    stacks = [
        jnp.concatenate([part[:, k * width : (k + 1) * width] for part in came], axis=0)
        for k in range(SIDE)
    ]
    return stacks[:1] + [along_dp(stacks[k], z_flip(k)) for k in range(1, SIDE)]


def sum_over_dp(array):
    for route in (x_flip(1), x_flip(2), z_flip(1), z_flip(2)):
        array = array + along_dp(array, route)
    return array


def stacked(rows_by_columns):
    count = rows_by_columns.shape[1] // HD
    return jnp.concatenate(
        [rows_by_columns[:, i * HD : (i + 1) * HD] for i in range(count)], axis=0
    )


def side_by_side(stack, rows):
    count = stack.shape[0] // rows
    return jnp.concatenate([stack[i * rows : (i + 1) * rows] for i in range(count)], axis=1)


def rope(vectors, cos_tab, sin_tab):
    return vectors * cos_tab + pltpu.roll(vectors, HD // 2, 1) * sin_tab


def unrope(vectors, cos_tab, sin_tab):
    return vectors * cos_tab - pltpu.roll(vectors, HD // 2, 1) * sin_tab


def head_norm(raw):
    inverse = lax.rsqrt(jnp.mean(raw * raw, axis=-1, keepdims=True) + EPSILON)
    return raw * inverse, inverse


def unit_back(grad_unit, unit, inverse):
    return inverse * (grad_unit - unit * jnp.mean(grad_unit * unit, axis=-1, keepdims=True))


def dot(a, b, a_dim, b_dim):
    return lax.dot_general(a, b, (((a_dim,), (b_dim,)), ((), ())), preferred_element_type=F32)


def attend(raw, gains, cos_tab, sin_tab, q_width):
    rows = raw.shape[0]
    q_unit, q_inv = head_norm(stacked(raw[:, :q_width]))
    k_unit, k_inv = head_norm(raw[:, q_width : q_width + HD])
    query = rope(q_unit * gains[0:1], cos_tab, sin_tab).astype(BF16)
    key = rope(k_unit * gains[1:2], cos_tab[:rows], sin_tab[:rows]).astype(BF16)
    value = raw[:, q_width + HD :].astype(BF16)
    scores = dot(query, key, 1, 1) * (1.0 / math.sqrt(HD))
    position = lax.broadcasted_iota(jnp.int32, scores.shape, 0) & (rows - 1)
    causal = position >= lax.broadcasted_iota(jnp.int32, scores.shape, 1)
    raised = jnp.where(causal, jnp.exp(scores), 0.0)
    probs = raised / jnp.sum(raised, axis=-1, keepdims=True)
    probs_b = probs.astype(BF16)
    attn = dot(probs_b, value, 1, 0).astype(BF16)
    return q_unit, q_inv, k_unit, k_inv, query, key, value, probs, probs_b, attn


def columns_of(activations, weights_ref, src_ref, out_ref, top, first, last):
    rows = activations.shape[0]
    width = out_ref.shape[1] // SIDE

    def group(i, carry):
        at = pl.multiple_of(src_ref[i] * width, width)
        here = pl.ds(pl.multiple_of(i * width, width), width)
        product = dot(activations, weights_ref[here, first:last], 1, 1).astype(BF16)
        out_ref[top : top + rows, pl.ds(at, width)] = product
        return carry

    lax.fori_loop(0, SIDE, group, 0)


def rows_of(rows_ref, weights_ref, src_ref, sum_ref, first, last):
    width = rows_ref.shape[1] // SIDE
    sum_ref[...] = jnp.zeros(sum_ref.shape, F32)

    def group(i, carry):
        at = pl.multiple_of(src_ref[i] * width, width)
        here = pl.ds(pl.multiple_of(i * width, width), width)
        sum_ref[...] += dot(rows_ref[:, pl.ds(at, width)], weights_ref[here, first:last], 1, 0)
        return carry

    lax.fori_loop(0, SIDE, group, 0)


def back_attention(raw, d_attn, gains, cos_tab, sin_tab, terms_ref):
    rows = raw.shape[0]
    q_unit, q_inv, k_unit, k_inv, query, key, value, probs, probs_b, attn = attend(
        raw, gains, cos_tab, sin_tab, d_attn.shape[1]
    )
    d_attn = stacked(d_attn)
    d_probs = dot(d_attn, value, 1, 1)
    d_value = dot(probs_b, d_attn, 0, 0).astype(BF16)
    d_scores = (
        probs
        * (d_probs - jnp.sum(probs * d_probs, axis=-1, keepdims=True))
        * (1.0 / math.sqrt(HD))
    ).astype(BF16)
    dq_r = unrope(dot(d_scores, key, 1, 0), cos_tab, sin_tab)
    dk_r = unrope(dot(d_scores, query, 0, 0), cos_tab[:rows], sin_tab[:rows])
    terms_ref[0:1, :] = jnp.sum(dq_r * q_unit, axis=0, keepdims=True)
    terms_ref[1:2, :] = jnp.sum(dk_r * k_unit, axis=0, keepdims=True)
    q_grad = unit_back(dq_r * gains[0:1], q_unit, q_inv).astype(BF16)
    k_grad = unit_back(dk_r * gains[1:2], k_unit, k_inv).astype(BF16)
    columns = jnp.concatenate([side_by_side(q_grad, rows), k_grad, d_value], axis=1)
    return side_by_side(attn, rows), columns


TILE = 16


def put_group(step, pieces, src_ref, weights_ref):
    size = pieces[0].shape[0]
    places = [(0, 0), (1, 0), (3, 0), (2, 0), (2, pieces[3].shape[0])]
    for piece, (flip, down) in zip(pieces, places):
        top = (step * SIDE + (src_ref[X_AT] ^ flip)) * size + down

        def put(i, carry, piece=piece, top=top):
            here = pl.multiple_of(i * TILE, TILE)
            there = pl.multiple_of(top + i * TILE, TILE)
            weights_ref[pl.ds(there, TILE), :] = piece[pl.ds(here, TILE), :]
            return carry

        lax.fori_loop(0, piece.shape[0] // TILE, put, 0)


def three_groups_kernel(src_ref, *refs):
    *pieces, weights_ref = refs
    put_group(0, pieces[:5], src_ref, weights_ref)
    put_group(1, pieces[5:9], src_ref, weights_ref)
    put_group(2, pieces[9:13], src_ref, weights_ref)


def first_kernel(
    src_ref, normed_ref, cot_ref, gains_ref, cos_ref, sin_ref, s0, s1, s2, s3, three_ref,
    parts_ref, early_ref, terms_ref, raw_2_ref, weights_ref, raw_ref, d_attn_ref,
):
    put_group(3, (s0, s1, s2, s3), src_ref, weights_ref)
    rows, q_width = d_attn_ref.shape
    in_width = raw_ref.shape[1]
    total = weights_ref.shape[1]
    rows_of(normed_ref, weights_ref, src_ref, raw_ref, 0, in_width)
    rows_of(cot_ref, weights_ref, src_ref, d_attn_ref, in_width, total)
    raw_2_ref[...] = raw_ref[2 * rows :, :]
    tables = (gains_ref[...], cos_ref[...], sin_ref[...])
    attn_1, columns = back_attention(
        raw_ref[:rows, :], d_attn_ref[...].astype(BF16), *tables, terms_ref
    )
    attn_f = side_by_side(attend(raw_ref[rows : 2 * rows, :], *tables, q_width)[-1], rows)
    attn_2 = side_by_side(attend(raw_ref[2 * rows :, :], *tables, q_width)[-1], rows)
    early_ref[:, :in_width] = columns
    early_ref[:, in_width : in_width + q_width] = attn_1
    early_ref[:, in_width + q_width :] = attn_2
    columns_of(attn_f, weights_ref, src_ref, parts_ref, 0, in_width, total)
    columns_of(columns, weights_ref, src_ref, parts_ref, rows, 0, in_width)


def prepare_kernel(
    info_ref, first_ref, second_ref, x_ref, cot_ref, scale_ref, normed_ref, p0, p1, p2, p3
):
    rows, features = cot_ref.shape
    for i, saved in enumerate((first_ref, x_ref, second_ref)):
        normed_ref[i * rows : (i + 1) * rows, :] = input_norm(saved[...], scale_ref[...])[2]
    width = features // (SIDE * SIDE)
    for j, part in enumerate((p0, p1, p2, p3)):
        for k in range(SIDE):
            replica = (info_ref[Z_AT] ^ k) * SIDE + (info_ref[X_AT] ^ j)
            here = pl.ds(pl.multiple_of(replica * width, width), width)
            at = 3 * k * width
            part[:, at : at + width] = normed_ref[0:rows, here]
            part[:, at + width : at + 2 * width] = normed_ref[2 * rows : 3 * rows, here]
            part[:, at + 2 * width : at + 3 * width] = cot_ref[:, here]


def backward_kernel(
    src_ref, raw_ref, cot_ref, gains_ref, cos_ref, sin_ref, weights_ref,
    c0, c1, c2, c3, part_ref, terms_ref, d_attn_ref,
):
    features = cot_ref.shape[1]
    in_width = raw_ref.shape[1]
    rows_of(cot_ref, weights_ref, src_ref, d_attn_ref, in_width, weights_ref.shape[1])
    columns = back_attention(
        raw_ref[...], d_attn_ref[...].astype(BF16), gains_ref[...], cos_ref[...], sin_ref[...],
        terms_ref,
    )[1]
    width = features // SIDE
    for k, payload in enumerate((c0, c1, c2, c3)):
        payload[:, :in_width] = columns
        at = pl.multiple_of((src_ref[Z_AT] ^ k) * width, width)
        payload[:, in_width:] = cot_ref[:, pl.ds(at, width)]
    columns_of(columns, weights_ref, src_ref, part_ref, 0, 0, in_width)


def spread_kernel(info_ref, c0, c1, c2, c3, mine_ref, near_ref, wrap_ref):
    rows = c0.shape[0]
    in_width = mine_ref.shape[1] - HD
    for k, part in enumerate((c0, c1, c2, c3)):
        here = slice(k * rows, (k + 1) * rows)
        for out_ref, flips in ((mine_ref, (0,)), (near_ref, (1, 2)), (wrap_ref, (3, 2))):
            out_ref[here, :in_width] = part[:, :in_width]
            for i, j in enumerate(flips):
                at = pl.multiple_of(in_width + (info_ref[X_AT] ^ j) * HD, HD)
                to = in_width + i * HD
                out_ref[here, to : to + HD] = part[:, pl.ds(at, HD)]


def forward_kernel(
    src_ref, x_ref, scale_ref, gains_ref, cos_ref, sin_ref, weights_ref,
    part_ref, normed_ref, raw_ref,
):
    rows = x_ref.shape[0]
    in_width = raw_ref.shape[1]
    total = weights_ref.shape[1]
    normed_ref[...] = input_norm(x_ref[...], scale_ref[...])[2]
    rows_of(normed_ref, weights_ref, src_ref, raw_ref, 0, in_width)
    attn = attend(raw_ref[...], gains_ref[...], cos_ref[...], sin_ref[...], total - in_width)[-1]
    columns_of(side_by_side(attn, rows), weights_ref, src_ref, part_ref, 0, in_width, total)


def post_kernel(
    core_ref, own_ref, other_ref, x_ref, cot_ref, saved_ref, scale_ref,
    out_ref, grad_ref, passed_ref, norm_ref,
):
    rows = x_ref.shape[0]
    sums = own_ref[...].astype(F32) + other_ref[...].astype(F32)
    out = (x_ref[...].astype(F32) + sums[:rows]).astype(BF16)
    inverse, unit, _ = input_norm(saved_ref[...], scale_ref[...])
    d_normed = sums[rows:]
    back = unit_back(d_normed * scale_ref[...], unit, inverse)
    grad = (cot_ref[...].astype(F32) + back).astype(BF16)
    out_ref[...] = out
    grad_ref[...] = grad
    norm_ref[...] = jnp.sum(d_normed * unit, axis=0, keepdims=True)

    @pl.when(core_ref[CORE_AT] == 0)
    def _():
        passed_ref[...] = out

    @pl.when(core_ref[CORE_AT] != 0)
    def _():
        passed_ref[...] = grad


def weights_kernel(
    info_ref, n0, n1, n2, n3, e0, e1, e2, e3, e4, l0, l1, l2, l3, l4,
    query_ref, key_ref, value_ref, out_ref, features_ref, *, scale
):
    rows = n0.shape[0] // SIDE
    q_width = query_ref.shape[2]
    in_width = q_width + 2 * HD
    for i, (j, k) in enumerate(FLIPS):
        for c in range(3):
            features_ref[c, i * rows : (i + 1) * rows, :] = (n0, n1, n2, n3)[k][
                j * rows : (j + 1) * rows, c * HD : (c + 1) * HD
            ]
    grad_in, grad_out, at = 0.0, 0.0, 0
    for i, (early, late) in enumerate(zip((e0, e1, e2, e3, e4), (l0, l1, l2, l3, l4))):
        here = slice(at, at + early.shape[0])
        at += early.shape[0]
        cot_at = in_width + (HD if i > 2 else 0)
        grad_in += dot(features_ref[0, here, :], early[:, :in_width], 0, 0)
        grad_in += dot(features_ref[1, here, :], late[:, :in_width], 0, 0)
        grad_out += dot(features_ref[2, here, :], early[:, in_width : in_width + q_width], 0, 0)
        grad_out += dot(late[:, cot_at : cot_at + HD], early[:, in_width + q_width :], 0, 0)
    query_ref[0] = scale * grad_in[:, :q_width]
    key_ref[0] = scale * grad_in[:, q_width : q_width + HD]
    value_ref[0] = scale * grad_in[:, q_width + HD :]
    out_ref[0] = scale * grad_out


def kernel_call(kernel, out_shape, *operands, scratch=(), aliases=None):
    spec = [pl.BlockSpec(memory_space=pltpu.SMEM)]
    spec += [pl.BlockSpec(memory_space=pltpu.VMEM)] * (len(operands) - 1)
    return pl.pallas_call(
        kernel,
        in_specs=spec,
        out_specs=jax.tree.map(lambda _: pl.BlockSpec(memory_space=pltpu.VMEM), out_shape),
        out_shape=out_shape,
        scratch_shapes=scratch,
        input_output_aliases=aliases or {},
        compiler_params=pltpu.CompilerParams(vmem_limit_bytes=VMEM_LIMIT),
        interpret=INTERPRET,
    )(*operands)


def rope_tables(length, copies):
    half_width = HD // 2
    freqs = jnp.exp(jnp.arange(half_width, dtype=F32) * (-2.0 * math.log(THETA) / HD))
    angles = jnp.arange(length, dtype=F32)[:, None] * freqs[None, :]
    cos_half, sin_half = jnp.cos(angles), jnp.sin(angles)
    cos_tab = jnp.concatenate([cos_half, cos_half], axis=1)
    sin_tab = jnp.concatenate([-sin_half, sin_half], axis=1)
    return jnp.tile(cos_tab, (copies, 1)), jnp.tile(sin_tab, (copies, 1))


def input_norm(rows, norm_scale):
    wide = rows.astype(F32)
    inverse = lax.rsqrt(jnp.mean(wide * wide, axis=-1, keepdims=True) + EPSILON)
    unit = wide * inverse
    return inverse, unit, (unit * norm_scale).astype(BF16)


def local(
    fwd_input,
    fresh_input,
    cotangent,
    fresh_cotangent,
    stash,
    norm_gain,
    qk_gain,
    w_query,
    w_key,
    w_value,
    w_out,
):
    replica = lax.axis_index("dp")
    z, x = replica // SIDE, replica % SIDE
    section = lax.axis_index("section")
    sections = lax.axis_size("section")
    core = lax.axis_index("tensor")
    q_width = w_query.shape[2]
    in_width = q_width + w_key.shape[2] + w_value.shape[2]
    rows = fwd_input.shape[1]
    norm_scale, gains = norm_gain[0], qk_gain[0]
    cos_tab, sin_tab = rope_tables(rows, q_width // HD)
    tables = (gains, cos_tab, sin_tab)

    shard = jnp.concatenate([w_query[0], w_key[0], w_value[0], w_out[0]], axis=1)
    total_width = shard.shape[1]
    pieces, sources = gather_weights(shard, z)
    info = jnp.concatenate([sources, jnp.stack([z, x, core])])
    mirror = [(s, sections - 1 - s) for s in range(sections)]
    fetched = lax.ppermute(jnp.where(core == 0, stash[0, 0], stash[0, 1]), "section", mirror)
    shared = other_core(fetched)
    reloaded = jnp.where(core == 0, fetched, shared), jnp.where(core == 0, shared, fetched)
    features = fwd_input.shape[2]
    width = features // SIDE

    def input_grad(cot_rows, d_normed, unit, inverse):
        back = unit_back(d_normed * norm_scale, unit, inverse)
        return (cot_rows.astype(F32) + back).astype(BF16)

    x_first, cot_first = fwd_input[0], cotangent[0]
    inv_2, unit_2, _ = input_norm(reloaded[1], norm_scale)
    parted = jax.ShapeDtypeStruct((rows, 3 * features // SIDE), BF16)
    normed, *parted = kernel_call(
        prepare_kernel,
        (jax.ShapeDtypeStruct((3 * rows, features), BF16), parted, parted, parted, parted),
        info, *reloaded, x_first, cot_first, norm_gain,
    )
    early = own_features(sent_along_x(parted))
    whole = jax.ShapeDtypeStruct((features, total_width), BF16)
    gate = pieces[2][3]
    first_three = [held_until(piece, gate) for group in pieces[:2] for piece in group[3:]]
    three = kernel_call(
        three_groups_kernel, whole, info,
        *pieces[0][:3], *first_three[:2], *pieces[1][:3], first_three[2], *pieces[2],
    )
    parts, early_block, terms_1, raw_2, weights = kernel_call(
        first_kernel,
        (
            jax.ShapeDtypeStruct((2 * rows, features), BF16),
            jax.ShapeDtypeStruct((rows, in_width + 2 * q_width), BF16),
            jax.ShapeDtypeStruct((2, HD), F32),
            jax.ShapeDtypeStruct((rows, in_width), F32),
            whole,
        ),
        info, normed, cot_first, *tables, *pieces[3], three,
        aliases={10: 4},
        scratch=[pltpu.VMEM((3 * rows, in_width), F32), pltpu.VMEM((rows, q_width), F32)],
    )
    block = jax.ShapeDtypeStruct((rows, features), BF16)
    out_first, grad_first, passed, norm_term_1 = kernel_call(
        post_kernel,
        (block, block, block, jax.ShapeDtypeStruct((1, features), F32)),
        info, parts, other_core(parts),
        x_first, cot_first, reloaded[0], norm_gain,
    )

    onward = [(2 * s, 2 * s + 2) for s in range(sections - 1)]
    back = [(2 * s + 1, 2 * s - 1) for s in range(1, sections)]
    passed = lax.ppermute(passed, ("section", "tensor"), onward + back)
    passed = jnp.where((core == 0) & (section == 0), fresh_input, passed)
    passed = jnp.where((core == 1) & (section == sections - 1), fresh_cotangent, passed)
    swapped = other_core(passed)
    x_second = jnp.where(core == 0, passed, swapped)
    cot_second = jnp.where(core == 0, swapped, passed)

    payload = jax.ShapeDtypeStruct((rows, in_width + width), BF16)
    *payloads, back_part, terms_2 = kernel_call(
        backward_kernel,
        (payload, payload, payload, payload, block, jax.ShapeDtypeStruct((2, HD), F32)),
        info, raw_2, cot_second, *tables, weights,
        scratch=[pltpu.VMEM((rows, q_width), F32)],
    )
    early_rows = gather_rows(early_block, passed)
    out_part = kernel_call(
        forward_kernel,
        block,
        info, x_second, norm_gain, *tables, weights,
        scratch=[pltpu.VMEM((rows, features), BF16), pltpu.VMEM((rows, in_width), F32)],
    )
    parts = lax.optimization_barrier(jnp.concatenate([out_part, back_part], axis=0))
    others = other_core(parts)
    sums = parts.astype(F32) + others.astype(F32)
    out_second = (x_second.astype(F32) + sums[:rows]).astype(BF16)
    d_normed_2 = sums[rows:]
    grad_second = input_grad(cot_second, d_normed_2, unit_2, inv_2)
    flips = [along_dp(payloads[k], z_flip(k)) for k in range(1, SIDE)]
    flips = [held_until(flip, others) for flip in flips]
    onto_x = jax.ShapeDtypeStruct((SIDE * rows, in_width + 2 * HD), BF16)
    mine, to_near, to_wrap = kernel_call(
        spread_kernel,
        (jax.ShapeDtypeStruct((SIDE * rows, in_width + HD), BF16), onto_x, onto_x),
        info, payloads[0], *flips,
    )
    late_rows = mine, *spread_along_x(to_near, to_wrap)

    out_activations = jnp.stack([out_first, out_second])[None]
    grad_input = jnp.stack([grad_first, grad_second])[None]

    scale = 1.0 / math.sqrt(2 * rows * lax.axis_size("dp"))
    like = [jax.ShapeDtypeStruct(w.shape, F32) for w in (w_query, w_key, w_value, w_out)]
    grads = kernel_call(
        functools.partial(weights_kernel, scale=scale),
        tuple(like),
        info, *early, *early_rows, *late_rows,
        scratch=[pltpu.VMEM((3, rows * SIDE * SIDE, HD), BF16)],
    )

    norm_term = norm_term_1[0] + jnp.sum(d_normed_2 * unit_2, axis=0)
    qk_term = terms_1 + terms_2
    qk_term = qk_term + other_core(qk_term)
    total = sum_over_dp(jnp.concatenate([norm_term.reshape(-1, HD), qk_term], axis=0) * scale)
    return (
        out_activations,
        grad_input,
        *grads,
        total[:-2].reshape(1, -1),
        total[-2:][None],
    )


def solution(mesh):
    return jax.shard_map(
        local,
        mesh=mesh,
        in_specs=(
            P("section", "dp", None),
            P("dp", None),
            P("section", "dp", None),
            P("dp", None),
            P("section", None, "dp", None),
            P("section", None),
            P("section", None, None),
            P("section", "dp", "tensor"),
            P("section", "dp", "tensor"),
            P("section", "dp", "tensor"),
            P("section", "dp", "tensor"),
        ),
        out_specs=(
            P("section", None, "dp", None),
            P("section", None, "dp", None),
            P("section", "dp", "tensor"),
            P("section", "dp", "tensor"),
            P("section", "dp", "tensor"),
            P("section", "dp", "tensor"),
            P("section", None),
            P("section", None, None),
        ),
        check_vma=False,
    )
```

profile of v0, /device:TPU:1, one launch (start us, length us, event | category | flops | bytes accessed | tf_op | source)
XLA Modules:
  0.0 202.6 jit_solution(12797558198071808491)
XLA Ops:
  1.8 2.5 %collective-permute-start.2 = (bf16[128,2304]{1,0:T(8,128)(2,1)S(1)}, bf16[128,2304]{1,0:T(8,128)(2,1)S(1)}, u32[]{:S(2)}, u32[]{:S(2)}) collective-permute-start(bf16[128,2304]{1,0:T(8,128)(2,1)S(1)} %pad_maximum_fusion.refs_0_), channel_id=1, source_target_pairs={{0,8},{2,10},{4,12},{6,14},{8,24},{10,26},{12,28},{14,30},{16,0},{... | collective-permute-start | bytes 1769480 | tf_op jit(solution)/shard_map/ppermute | solution.py:39
  4.3 13.0 %collective-permute-done.2.refs_5_ = bf16[128,2304]{1,0:T(8,128)(2,1)S(1)} collective-permute-done((bf16[128,2304]{1,0:T(8,128)(2,1)S(1)}, bf16[128,2304]{1,0:T(8,128)(2,1)S(1)}, u32[]{:S(2)}, u32[]{:S(2)}) %collective-permute-start.2) | collective-permute-done | bytes 589856 | tf_op jit(solution)/shard_map/ppermute | solution.py:39
  17.4 2.6 %collective-permute-start.7 = (bf16[128,2304]{1,0:T(8,128)(2,1)S(1)}, bf16[128,2304]{1,0:T(8,128)(2,1)S(1)}, u32[]{:S(2)}, u32[]{:S(2)}) collective-permute-start(bf16[128,2304]{1,0:T(8,128)(2,1)S(1)} %collective-permute-done.2.refs_5_), channel_id=1, source_target_pairs={{0,2},{2,0},{4,6},{6,4},{8,10},{10,8},{12,14},{14,12},{16,18},{18,... | collective-permute-start | bytes 1769480 | tf_op jit(solution)/shard_map/ppermute | solution.py:39
  19.9 8.5 %collective-permute-start = (bf16[32,2048]{1,0:T(8,128)(2,1)S(1)}, bf16[32,2048]{1,0:T(8,128)(2,1)S(1)}, u32[]{:S(2)}, u32[]{:S(2)}) collective-permute-start(bf16[32,2048]{1,0:T(8,128)(2,1)S(1)} %select_bitcast_fusion), channel_id=1, source_target_pairs={{0,224},{32,192},{64,160},{96,128},{128,96},{160,64},{192,32},{224... | collective-permute-start | bytes 393224 | tf_op jit(solution)/shard_map/ppermute | solution.py:441
  31.0 4.0 %collective-permute-start.1 = (bf16[32,2048]{1,0:T(8,128)(2,1)S(1)}, bf16[32,2048]{1,0:T(8,128)(2,1)S(1)}, u32[]{:S(2)}, u32[]{:S(2)}) collective-permute-start(bf16[32,2048]{1,0:T(8,128)(2,1)S(1)} %collective-permute-done), channel_id=1, source_target_pairs={{0,1},{1,0},{2,3},{3,2},{4,5},{5,4},{6,7},{7,6},{8,9},{9,8},{10,11... | collective-permute-start | bytes 393224 | tf_op jit(solution)/shard_map/ppermute | solution.py:43
  38.1 17.1 %collective-permute-done.9.refs_7_ = bf16[128,2304]{1,0:T(8,128)(2,1)S(1)} collective-permute-done((bf16[128,2304]{1,0:T(8,128)(2,1)S(1)}, bf16[128,2304]{1,0:T(8,128)(2,1)S(1)}, u32[]{:S(2)}, u32[]{:S(2)}) %collective-permute-start.9) | collective-permute-done | bytes 589856 | tf_op jit(solution)/shard_map/ppermute | solution.py:39
  55.4 6.1 %collective-permute-done.8 = bf16[64,2304]{1,0:T(8,128)(2,1)S(1)} collective-permute-done((bf16[64,2304]{1,0:T(8,128)(2,1)S(1)}, bf16[64,2304]{1,0:T(8,128)(2,1)S(1)}, u32[]{:S(2)}, u32[]{:S(2)}) %collective-permute-start.8) | collective-permute-done | bytes 294944 | tf_op jit(solution)/shard_map/ppermute | solution.py:39
  62.8 3.1 %collective-permute-start.24 = (bf16[32,1536]{1,0:T(8,128)(2,1)S(1)}, bf16[32,1536]{1,0:T(8,128)(2,1)S(1)}, u32[]{:S(2)}, u32[]{:S(2)}) collective-permute-start(bf16[32,1536]{1,0:T(8,128)(2,1)S(1)} %get-tuple-element.57), channel_id=1, source_target_pairs={{0,4},{2,6},{4,0},{6,2},{8,12},{10,14},{12,8},{14,10},{16,20},{18,... | collective-permute-start | bytes 294920 | tf_op jit(solution)/shard_map/ppermute | solution.py:39
  71.3 4.2 %collective-permute-done.25 = bf16[32,1536]{1,0:T(8,128)(2,1)S(1)} collective-permute-done((bf16[32,1536]{1,0:T(8,128)(2,1)S(1)}, bf16[32,1536]{1,0:T(8,128)(2,1)S(1)}, u32[]{:S(2)}, u32[]{:S(2)}) %collective-permute-start.25) | collective-permute-done | bytes 98336 | tf_op jit(solution)/shard_map/ppermute | solution.py:39
  75.5 2.9 %collective-permute-start.18 = (bf16[128,2304]{1,0:T(8,128)(2,1)S(1)}, bf16[128,2304]{1,0:T(8,128)(2,1)S(1)}, u32[]{:S(2)}, u32[]{:S(2)}) collective-permute-start(bf16[128,2304]{1,0:T(8,128)(2,1)S(1)} %collective-permute-done.3.refs_9_), channel_id=1, source_target_pairs={{0,6},{2,4},{4,2},{6,0},{8,14},{10,12},{12,10},{14,8},{16,22},{18,... | collective-permute-start | bytes 1769480 | tf_op jit(solution)/shard_map/ppermute | solution.py:39
  80.0 9.5 %collective-permute-done.18.refs_11_ = bf16[128,2304]{1,0:T(8,128)(2,1)S(1)} collective-permute-done((bf16[128,2304]{1,0:T(8,128)(2,1)S(1)}, bf16[128,2304]{1,0:T(8,128)(2,1)S(1)}, u32[]{:S(2)}, u32[]{:S(2)}) %collective-permute-start.18) | collective-permute-done | bytes 589856 | tf_op jit(solution)/shard_map/ppermute | solution.py:39
  90.9 9.2 %collective-permute-done.6.s2 = bf16[128,2304]{1,0:T(8,128)(2,1)S(1)} collective-permute-done((bf16[128,2304]{1,0:T(8,128)(2,1)S(1)}, bf16[128,2304]{1,0:T(8,128)(2,1)S(1)}, u32[]{:S(2)}, u32[]{:S(2)}) %collective-permute-start.6) | collective-permute-done | bytes 589856 | tf_op jit(solution)/shard_map/ppermute | solution.py:39
  100.2 8.2 %shard_map.172 = (bf16[64,2048]{1,0:T(8,128)(2,1)S(1)}, bf16[32,3328]{1,0:T(8,128)(2,1)S(1)}, f32[2,128]{1,0:T(2,128)S(1)}, f32[32,1280]{1,0:T(8,128)S(1)}, bf16[2048,2304]{1,0:T(8,128)(2,1)S(1)}) custom-call(s32[7]{0:T(128)S(1)} %concatenate.36.info_ref.src_ref.core_ref, ...), custom_call_target="tpu_custom_call", output_to_operand_aliasing={{4}: (10, {})} | custom-call | tf_op jit(solution)/shard_map/pallas_call | solution.py:382
  108.4 9.2 %collective-permute-start.19 = (bf16[64,2048]{1,0:T(8,128)(2,1)S(1)}, bf16[64,2048]{1,0:T(8,128)(2,1)S(1)}, u32[]{:S(2)}, u32[]{:S(2)}) collective-permute-start(bf16[64,2048]{1,0:T(8,128)(2,1)S(1)} %get-tuple-element.48.own_ref), channel_id=1, source_target_pairs={{0,1},{1,0},{2,3},{3,2},{4,5},{5,4},{6,7},{7,6},{8,9},{9,8},{10,11... | collective-permute-start | bytes 786440 | tf_op jit(solution)/shard_map/ppermute | solution.py:43
  123.4 14.8 %collective-permute-done.20 = bf16[32,2048]{1,0:T(8,128)(2,1)S(1)} collective-permute-done((bf16[32,2048]{1,0:T(8,128)(2,1)S(1)}, bf16[32,2048]{1,0:T(8,128)(2,1)S(1)}, u32[]{:S(2)}, u32[]{:S(2)}) %collective-permute-start.20) | collective-permute-done | bytes 131104 | tf_op jit(solution)/shard_map/ppermute | solution.py:490
  138.4 4.5 %collective-permute-done.30 = bf16[32,3328]{1,0:T(8,128)(2,1)S(1)} collective-permute-done((bf16[32,3328]{1,0:T(8,128)(2,1)S(1)}, bf16[32,3328]{1,0:T(8,128)(2,1)S(1)}, u32[]{:S(2)}, u32[]{:S(2)}) %collective-permute-start.30) | collective-permute-done | bytes 213024 | tf_op jit(solution)/shard_map/ppermute | solution.py:39
  143.0 4.2 %shard_map.174 = bf16[32,2048]{1,0:T(8,128)(2,1)S(1)} custom-call(s32[7]{0:T(128)S(1)} %concatenate.36.info_ref.src_ref.core_ref, bf16[32,2048]{1,0:T(8,128)(2,1)S(1)} %get-tuple-element.86.x_ref, f32[1,2048]{1,0:T(1,128)S(1)} %copy-done.2, f32[2,128]{1,0:T(2,128)S(1)} %bitcast.50, f32[256,128]{1,0:T(8,128)S(1)} %bitcast.35, f32[256,128]{1,0:T(8,128)S(1)} %bitcast.38, ...), custom_call_target="tpu_custom_call" | custom-call | tf_op jit(solution)/shard_map/pallas_call | solution.py:382
  147.2 4.5 %shard_map.175 = (bf16[32,1792]{1,0:T(8,128)(2,1)S(1)}, bf16[32,1792]{1,0:T(8,128)(2,1)S(1)}, bf16[32,1792]{1,0:T(8,128)(2,1)S(1)}, bf16[32,1792]{1,0:T(8,128)(2...) custom-call(s32[7]{0:T(128)S(1)} %concatenate.36.info_ref.src_ref.core_ref, ...), custom_call_target="tpu_custom_call" | custom-call | tf_op jit(solution)/shard_map/pallas_call | solution.py:382
  161.0 5.5 %collective-permute-done.38.c3 = bf16[32,1792]{1,0:T(8,128)(2,1)S(1)} collective-permute-done((bf16[32,1792]{1,0:T(8,128)(2,1)S(1)}, bf16[32,1792]{1,0:T(8,128)(2,1)S(1)}, u32[]{:S(2)}, u32[]{:S(2)}) %collective-permute-start.38) | collective-permute-done | bytes 114720 | tf_op jit(solution)/shard_map/ppermute | solution.py:39
  168.7 8.4 %collective-permute-done.45 = f32[18,128]{1,0:T(8,128)S(1)} collective-permute-done((f32[18,128]{1,0:T(8,128)S(1)}, f32[18,128]{1,0:T(8,128)S(1)}, u32[]{:S(2)}, u32[]{:S(2)}) %collective-permute-start.45) | collective-permute-done | bytes 9248 | tf_op jit(solution)/shard_map/ppermute | solution.py:39
  177.2 2.0 %collective-permute-start.40 = (bf16[128,1536]{1,0:T(8,128)(2,1)S(1)}, bf16[128,1536]{1,0:T(8,128)(2,1)S(1)}, u32[]{:S(2)}, u32[]{:S(2)}) collective-permute-start(bf16[128,1536]{1,0:T(8,128)(2,1)S(1)} %get-tuple-element.72), channel_id=1, source_target_pairs={{0,6},{2,4},{4,2},{6,0},{8,14},{10,12},{12,10},{14,8},{16,22},{18,... | collective-permute-start | bytes 1179656 | tf_op jit(solution)/shard_map/ppermute | solution.py:39
  188.5 2.1 %collective-permute-start.41 = (bf16[64,1536]{1,0:T(8,128)(2,1)S(1)}, bf16[64,1536]{1,0:T(8,128)(2,1)S(1)}, u32[]{:S(2)}, u32[]{:S(2)}) collective-permute-start(bf16[64,1536]{1,0:T(8,128)(2,1)S(1)} %slice.161), channel_id=1, source_target_pairs={{0,6},{2,4},{4,2},{6,0},{8,14},{10,12},{12,10},{14,8},{16,22},{18,... | collective-permute-start | bytes 589832 | tf_op jit(solution)/shard_map/ppermute | solution.py:39
  192.7 6.6 %collective-permute-done.41.l3 = bf16[64,1536]{1,0:T(8,128)(2,1)S(1)} collective-permute-done((bf16[64,1536]{1,0:T(8,128)(2,1)S(1)}, bf16[64,1536]{1,0:T(8,128)(2,1)S(1)}, u32[]{:S(2)}, u32[]{:S(2)}) %collective-permute-start.41) | collective-permute-done | bytes 196640 | tf_op jit(solution)/shard_map/ppermute | solution.py:39
  199.4 3.2 %shard_map.177 = (f32[1,128,1024]{2,1,0:T(8,128)}, f32[1,128,128]{2,1,0:T(8,128)}, f32[1,128,128]{2,1,0:T(8,128)}, f32[1,128,1024]{2,1,0:T(8,128)}) custom-call(s32[7]{0:T(128)S(1)} %concatenate.36.info_ref.src_ref.core_ref, bf16[128,384]{1,0:T(8,128)(2,1)S(1)} %pad_maximum_fusion.2.n0, bf16[128,384]{1,0:T(8,128)(2,1)S(1)} %collective-permute-done.26.n1, ...), custom_call_target="tpu_custom_call" | custom-call | tf_op jit(solution)/shard_map/pallas_call | solution.py:382
  (146 shorter events, 45.5 us)
Async XLA Ops:
  1.8 15.6 %collective-permute-start.2 = (bf16[128,2304]{1,0:T(8,128)(2,1)S(1)}, bf16[128,2304]{1,0:T(8,128)(2,1)S(1)}, u32[]{:S(2)}, u32[]{:S(2)}) collective-permute-start(bf16[128,2304]{1,0:T(8,128)(2,1)S(1)} %pad_maximum_fusion.refs_0_), channel_id=1, source_target_pairs={{0,8},{2,10},{4,12},{6,14},{8,24},{10,26},{12,28},{14,30},{16,0},{... | collective-permute-start | bytes 1769480 | tf_op jit(solution)/shard_map/ppermute | solution.py:39
  17.4 19.5 %collective-permute-start.7 = (bf16[128,2304]{1,0:T(8,128)(2,1)S(1)}, bf16[128,2304]{1,0:T(8,128)(2,1)S(1)}, u32[]{:S(2)}, u32[]{:S(2)}) collective-permute-start(bf16[128,2304]{1,0:T(8,128)(2,1)S(1)} %collective-permute-done.2.refs_5_), channel_id=1, source_target_pairs={{0,2},{2,0},{4,6},{6,4},{8,10},{10,8},{12,14},{14,12},{16,18},{18,... | collective-permute-start | bytes 1769480 | tf_op jit(solution)/shard_map/ppermute | solution.py:39
  28.5 34.3 %collective-permute-start.14 = (bf16[128,2304]{1,0:T(8,128)(2,1)S(1)}, bf16[128,2304]{1,0:T(8,128)(2,1)S(1)}, u32[]{:S(2)}, u32[]{:S(2)}) collective-permute-start(bf16[128,2304]{1,0:T(8,128)(2,1)S(1)} %pad_maximum_fusion.refs_0_), channel_id=1, source_target_pairs={{0,6},{2,4},{4,2},{6,0},{8,14},{10,12},{12,10},{14,8},{16,22},{18,... | collective-permute-start | bytes 1769480 | tf_op jit(solution)/shard_map/ppermute | solution.py:39
  35.0 20.2 %collective-permute-start.9 = (bf16[128,2304]{1,0:T(8,128)(2,1)S(1)}, bf16[128,2304]{1,0:T(8,128)(2,1)S(1)}, u32[]{:S(2)}, u32[]{:S(2)}) collective-permute-start(bf16[128,2304]{1,0:T(8,128)(2,1)S(1)} %collective-permute-done.2.refs_5_), channel_id=1, source_target_pairs={{0,6},{2,4},{4,2},{6,0},{8,14},{10,12},{12,10},{14,8},{16,22},{18,... | collective-permute-start | bytes 1769480 | tf_op jit(solution)/shard_map/ppermute | solution.py:39
  36.8 18.5 %collective-permute-start.3 = (bf16[128,2304]{1,0:T(8,128)(2,1)S(1)}, bf16[128,2304]{1,0:T(8,128)(2,1)S(1)}, u32[]{:S(2)}, u32[]{:S(2)}) collective-permute-start(bf16[128,2304]{1,0:T(8,128)(2,1)S(1)} %collective-permute-done.2.refs_5_), channel_id=1, source_target_pairs={{0,8},{2,10},{4,12},{6,14},{8,24},{10,26},{12,28},{14,30},{16,0},{... | collective-permute-start | bytes 1769480 | tf_op jit(solution)/shard_map/ppermute | solution.py:39
  36.9 29.0 %collective-permute-start.13 = (bf16[128,2304]{1,0:T(8,128)(2,1)S(1)}, bf16[128,2304]{1,0:T(8,128)(2,1)S(1)}, u32[]{:S(2)}, u32[]{:S(2)}) collective-permute-start(bf16[128,2304]{1,0:T(8,128)(2,1)S(1)} %pad_maximum_fusion.refs_0_), channel_id=1, source_target_pairs={{0,2},{2,0},{4,6},{6,4},{8,10},{10,8},{12,14},{14,12},{16,18},{18,... | collective-permute-start | bytes 1769480 | tf_op jit(solution)/shard_map/ppermute | solution.py:39
  37.3 24.1 %collective-permute-start.8 = (bf16[64,2304]{1,0:T(8,128)(2,1)S(1)}, bf16[64,2304]{1,0:T(8,128)(2,1)S(1)}, u32[]{:S(2)}, u32[]{:S(2)}) collective-permute-start(bf16[64,2304]{1,0:T(8,128)(2,1)S(1)} %slice.138), channel_id=1, source_target_pairs={{0,6},{2,4},{4,2},{6,0},{8,14},{10,12},{12,10},{14,8},{16,22},{18,... | collective-permute-start | bytes 884744 | tf_op jit(solution)/shard_map/ppermute | solution.py:39
  55.3 23.1 %collective-permute-start.4 = (bf16[128,2304]{1,0:T(8,128)(2,1)S(1)}, bf16[128,2304]{1,0:T(8,128)(2,1)S(1)}, u32[]{:S(2)}, u32[]{:S(2)}) collective-permute-start(bf16[128,2304]{1,0:T(8,128)(2,1)S(1)} %collective-permute-done.3.refs_9_), channel_id=1, source_target_pairs={{0,8},{2,10},{4,12},{6,14},{8,24},{10,26},{12,28},{14,30},{16,0},{... | collective-permute-start | bytes 1769480 | tf_op jit(solution)/shard_map/ppermute | solution.py:39
  61.5 18.4 %collective-permute-start.11 = (bf16[128,2304]{1,0:T(8,128)(2,1)S(1)}, bf16[128,2304]{1,0:T(8,128)(2,1)S(1)}, u32[]{:S(2)}, u32[]{:S(2)}) collective-permute-start(bf16[128,2304]{1,0:T(8,128)(2,1)S(1)} %constant_dynamic-update-slice_fusion.refs_8_), channel_id=1, source_target_pairs={{0,8},{2,10},{4,12},{6,14},{8,24},{10,26},{12,28},{14,30},{16,0},{... | collective-permute-start | bytes 1769480 | tf_op jit(solution)/shard_map/ppermute | solution.py:39
  65.9 12.5 %collective-permute-start.16 = (bf16[64,2304]{1,0:T(8,128)(2,1)S(1)}, bf16[64,2304]{1,0:T(8,128)(2,1)S(1)}, u32[]{:S(2)}, u32[]{:S(2)}) collective-permute-start(bf16[64,2304]{1,0:T(8,128)(2,1)S(1)} %slice.142), channel_id=1, source_target_pairs={{0,2},{2,0},{4,6},{6,4},{8,10},{10,8},{12,14},{14,12},{16,18},{18,... | collective-permute-start | bytes 884744 | tf_op jit(solution)/shard_map/ppermute | solution.py:39
  75.5 14.0 %collective-permute-start.18 = (bf16[128,2304]{1,0:T(8,128)(2,1)S(1)}, bf16[128,2304]{1,0:T(8,128)(2,1)S(1)}, u32[]{:S(2)}, u32[]{:S(2)}) collective-permute-start(bf16[128,2304]{1,0:T(8,128)(2,1)S(1)} %collective-permute-done.3.refs_9_), channel_id=1, source_target_pairs={{0,6},{2,4},{4,2},{6,0},{8,14},{10,12},{12,10},{14,8},{16,22},{18,... | collective-permute-start | bytes 1769480 | tf_op jit(solution)/shard_map/ppermute | solution.py:39
  78.4 21.7 %collective-permute-start.6 = (bf16[128,2304]{1,0:T(8,128)(2,1)S(1)}, bf16[128,2304]{1,0:T(8,128)(2,1)S(1)}, u32[]{:S(2)}, u32[]{:S(2)}) collective-permute-start(bf16[128,2304]{1,0:T(8,128)(2,1)S(1)} %collective-permute-done.4.s0), channel_id=1, source_target_pairs={{0,6},{2,4},{4,2},{6,0},{8,14},{10,12},{12,10},{14,8},{16,22},{18,... | collective-permute-start | bytes 1769480 | tf_op jit(solution)/shard_map/ppermute | solution.py:39
  78.5 21.6 %collective-permute-start.5 = (bf16[128,2304]{1,0:T(8,128)(2,1)S(1)}, bf16[128,2304]{1,0:T(8,128)(2,1)S(1)}, u32[]{:S(2)}, u32[]{:S(2)}) collective-permute-start(bf16[128,2304]{1,0:T(8,128)(2,1)S(1)} %collective-permute-done.4.s0), channel_id=1, source_target_pairs={{0,2},{2,0},{4,6},{6,4},{8,10},{10,8},{12,14},{14,12},{16,18},{18,... | collective-permute-start | bytes 1769480 | tf_op jit(solution)/shard_map/ppermute | solution.py:39
  79.9 20.2 %collective-permute-start.12 = (bf16[128,2304]{1,0:T(8,128)(2,1)S(1)}, bf16[128,2304]{1,0:T(8,128)(2,1)S(1)}, u32[]{:S(2)}, u32[]{:S(2)}) collective-permute-start(bf16[128,2304]{1,0:T(8,128)(2,1)S(1)} %collective-permute-done.11.refs_12_), channel_id=1, source_target_pairs={{0,8},{2,10},{4,12},{6,14},{8,24},{10,26},{12,28},{14,30},{16,0},{... | collective-permute-start | bytes 1769480 | tf_op jit(solution)/shard_map/ppermute | solution.py:39
  108.4 12.9 %collective-permute-start.19 = (bf16[64,2048]{1,0:T(8,128)(2,1)S(1)}, bf16[64,2048]{1,0:T(8,128)(2,1)S(1)}, u32[]{:S(2)}, u32[]{:S(2)}) collective-permute-start(bf16[64,2048]{1,0:T(8,128)(2,1)S(1)} %get-tuple-element.48.own_ref), channel_id=1, source_target_pairs={{0,1},{1,0},{2,3},{3,2},{4,5},{5,4},{6,7},{7,6},{8,9},{9,8},{10,11... | collective-permute-start | bytes 786440 | tf_op jit(solution)/shard_map/ppermute | solution.py:43
  117.6 35.2 %collective-permute-start.31 = (bf16[32,3328]{1,0:T(8,128)(2,1)S(1)}, bf16[32,3328]{1,0:T(8,128)(2,1)S(1)}, u32[]{:S(2)}, u32[]{:S(2)}) collective-permute-start(bf16[32,3328]{1,0:T(8,128)(2,1)S(1)} %get-tuple-element.59), channel_id=1, source_target_pairs={{0,24},{2,26},{4,28},{6,30},{8,16},{10,18},{12,20},{14,22},{16,8},... | collective-permute-start | bytes 638984 | tf_op jit(solution)/shard_map/ppermute | solution.py:39
  119.3 23.6 %collective-permute-start.30 = (bf16[32,3328]{1,0:T(8,128)(2,1)S(1)}, bf16[32,3328]{1,0:T(8,128)(2,1)S(1)}, u32[]{:S(2)}, u32[]{:S(2)}) collective-permute-start(bf16[32,3328]{1,0:T(8,128)(2,1)S(1)} %get-tuple-element.59), channel_id=1, source_target_pairs={{0,16},{2,18},{4,20},{6,22},{8,24},{10,26},{12,28},{14,30},{16,0},... | collective-permute-start | bytes 638984 | tf_op jit(solution)/shard_map/ppermute | solution.py:39
  119.7 18.7 %collective-permute-start.29 = (bf16[32,3328]{1,0:T(8,128)(2,1)S(1)}, bf16[32,3328]{1,0:T(8,128)(2,1)S(1)}, u32[]{:S(2)}, u32[]{:S(2)}) collective-permute-start(bf16[32,3328]{1,0:T(8,128)(2,1)S(1)} %get-tuple-element.59), channel_id=1, source_target_pairs={{0,8},{2,10},{4,12},{6,14},{8,0},{10,2},{12,4},{14,6},{16,24},{18,... | collective-permute-start | bytes 638984 | tf_op jit(solution)/shard_map/ppermute | solution.py:39
  122.1 16.1 %collective-permute-start.20 = (bf16[32,2048]{1,0:T(8,128)(2,1)S(1)}, bf16[32,2048]{1,0:T(8,128)(2,1)S(1)}, u32[]{:S(2)}, u32[]{:S(2)}) collective-permute-start(bf16[32,2048]{1,0:T(8,128)(2,1)S(1)} %get-tuple-element.50), channel_id=1, source_target_pairs={{0,32},{32,64},{64,96},{96,128},{128,160},{160,192},{192,224},{33,... | collective-permute-start | bytes 393224 | tf_op jit(solution)/shard_map/ppermute | solution.py:490
  154.7 27.2 %collective-permute-start.33 = (bf16[128,3328]{1,0:T(8,128)(2,1)S(1)}, bf16[128,3328]{1,0:T(8,128)(2,1)S(1)}, u32[]{:S(2)}, u32[]{:S(2)}) collective-permute-start(bf16[128,3328]{1,0:T(8,128)(2,1)S(1)} %constant_dynamic-update-slice_fusion.2.e0), channel_id=1, source_target_pairs={{0,6},{2,4},{4,2},{6,0},{8,14},{10,12},{12,10},{14,8},{16,22},{18,... | collective-permute-start | bytes 2555912 | tf_op jit(solution)/shard_map/ppermute | solution.py:39
  156.6 26.0 %collective-permute-start.32 = (bf16[128,3328]{1,0:T(8,128)(2,1)S(1)}, bf16[128,3328]{1,0:T(8,128)(2,1)S(1)}, u32[]{:S(2)}, u32[]{:S(2)}) collective-permute-start(bf16[128,3328]{1,0:T(8,128)(2,1)S(1)} %constant_dynamic-update-slice_fusion.2.e0), channel_id=1, source_target_pairs={{0,2},{2,0},{4,6},{6,4},{8,10},{10,8},{12,14},{14,12},{16,18},{18,... | collective-permute-start | bytes 2555912 | tf_op jit(solution)/shard_map/ppermute | solution.py:39
  168.5 16.9 %collective-permute-start.39 = (bf16[128,1536]{1,0:T(8,128)(2,1)S(1)}, bf16[128,1536]{1,0:T(8,128)(2,1)S(1)}, u32[]{:S(2)}, u32[]{:S(2)}) collective-permute-start(bf16[128,1536]{1,0:T(8,128)(2,1)S(1)} %get-tuple-element.71), channel_id=1, source_target_pairs={{0,2},{2,0},{4,6},{6,4},{8,10},{10,8},{12,14},{14,12},{16,18},{18,... | collective-permute-start | bytes 1179656 | tf_op jit(solution)/shard_map/ppermute | solution.py:39
  184.0 15.4 %collective-permute-start.35 = (bf16[64,3328]{1,0:T(8,128)(2,1)S(1)}, bf16[64,3328]{1,0:T(8,128)(2,1)S(1)}, u32[]{:S(2)}, u32[]{:S(2)}) collective-permute-start(bf16[64,3328]{1,0:T(8,128)(2,1)S(1)} %slice.159), channel_id=1, source_target_pairs={{0,2},{2,0},{4,6},{6,4},{8,10},{10,8},{12,14},{14,12},{16,18},{18,... | collective-permute-start | bytes 1277960 | tf_op jit(solution)/shard_map/ppermute | solution.py:39
  185.4 14.0 %collective-permute-start.34 = (bf16[64,3328]{1,0:T(8,128)(2,1)S(1)}, bf16[64,3328]{1,0:T(8,128)(2,1)S(1)}, u32[]{:S(2)}, u32[]{:S(2)}) collective-permute-start(bf16[64,3328]{1,0:T(8,128)(2,1)S(1)} %slice.158), channel_id=1, source_target_pairs={{0,6},{2,4},{4,2},{6,0},{8,14},{10,12},{12,10},{14,8},{16,22},{18,... | collective-permute-start | bytes 1277960 | tf_op jit(solution)/shard_map/ppermute | solution.py:39
  (31 other events, 341.9 us)
where the time goes:
time: 205 us; the launch traced here: 203 us
  waiting for transfers between devices  107 us (52%)
  starting transfers between devices  66 us (32%)
  Pallas kernels  23.8 us (12%)
  other arithmetic  3.56 us (2%)
    ppermute x41, waiting for transfers between devices, along_dp(): return lax.ppermute(array, 'dp', route)  89.7 us
    ppermute x41, starting transfers between devices, along_dp(): return lax.ppermute(array, 'dp', route)  41.9 us
    pallas_call x8, Pallas kernels, kernel_call(): pl.pallas_call(kernel, in_specs=spec, out_specs=jax.tree.map(lambda _: pl...  23.8 us
    ppermute x1, waiting for transfers between devices, local(): passed = lax.ppermute(passed, ('section', 'tensor'), onward + back)  14.8 us
    ppermute x5, starting transfers between devices, other_core(): return lax.ppermute(array, 'tensor', [(0, 1), (1, 0)])  14.3 us
    ppermute x1, starting transfers between devices, local(): lax.ppermute(jnp.where(core == 0, stash[0, 0], stash[0, 1]), 'section', m...  8.53 us
  transfers between devices with their start and end apart: 48, of which 19 were waited for; matrix products, arithmetic and copies ran while one was open for 2% of the time, Pallas kernels for 6%

commit v1 on v0

--- a/solution.py
+++ b/solution.py
@@ -17,7 +17,7 @@
 BF16 = jnp.bfloat16
 INTERPRET = False
 Z_AT, X_AT, CORE_AT = 4, 5, 6
-VMEM_LIMIT = 16 * 1024 * 1024
+VMEM_LIMIT = 10 * 1024 * 1024
 
 
 LINE_RING = {0: 1, 1: 3, 3: 2, 2: 0}
@@ -178,9 +178,8 @@
     lax.fori_loop(0, SIDE, group, 0)
 
 
-def rows_of(rows_ref, weights_ref, src_ref, sum_ref, first, last):
+def rows_of(rows_ref, weights_ref, src_ref, sum_ref, first, last, groups):
     width = rows_ref.shape[1] // SIDE
-    sum_ref[...] = jnp.zeros(sum_ref.shape, F32)
 
     def group(i, carry):
         at = pl.multiple_of(src_ref[i] * width, width)
@@ -188,7 +187,7 @@
         sum_ref[...] += dot(rows_ref[:, pl.ds(at, width)], weights_ref[here, first:last], 1, 0)
         return carry
 
-    lax.fori_loop(0, SIDE, group, 0)
+    lax.fori_loop(*groups, group, 0)
 
 
 def back_attention(raw, d_attn, gains, cos_tab, sin_tab, terms_ref):
@@ -232,23 +231,31 @@
         lax.fori_loop(0, piece.shape[0] // TILE, put, 0)
 
 
-def three_groups_kernel(src_ref, *refs):
-    *pieces, weights_ref = refs
+def three_groups_kernel(src_ref, normed_ref, cot_ref, *refs):
+    *pieces, weights_ref, raw_ref, d_attn_ref = refs
     put_group(0, pieces[:5], src_ref, weights_ref)
     put_group(1, pieces[5:9], src_ref, weights_ref)
     put_group(2, pieces[9:13], src_ref, weights_ref)
+    in_width, total = raw_ref.shape[1], weights_ref.shape[1]
+    raw_ref[...] = jnp.zeros(raw_ref.shape, F32)
+    d_attn_ref[...] = jnp.zeros(d_attn_ref.shape, F32)
+    rows_of(normed_ref, weights_ref, src_ref, raw_ref, 0, in_width, (0, 3))
+    rows_of(cot_ref, weights_ref, src_ref, d_attn_ref, in_width, total, (0, 3))
 
 
 def first_kernel(
-    src_ref, normed_ref, cot_ref, gains_ref, cos_ref, sin_ref, s0, s1, s2, s3, three_ref,
+    src_ref, normed_ref, cot_ref, gains_ref, cos_ref, sin_ref, raw_3_ref, d_attn_3_ref,
+    s0, s1, s2, s3, three_ref,
     parts_ref, early_ref, terms_ref, raw_2_ref, weights_ref, raw_ref, d_attn_ref,
 ):
     put_group(3, (s0, s1, s2, s3), src_ref, weights_ref)
     rows, q_width = d_attn_ref.shape
     in_width = raw_ref.shape[1]
     total = weights_ref.shape[1]
-    rows_of(normed_ref, weights_ref, src_ref, raw_ref, 0, in_width)
-    rows_of(cot_ref, weights_ref, src_ref, d_attn_ref, in_width, total)
+    raw_ref[...] = raw_3_ref[...]
+    d_attn_ref[...] = d_attn_3_ref[...]
+    rows_of(normed_ref, weights_ref, src_ref, raw_ref, 0, in_width, (3, 4))
+    rows_of(cot_ref, weights_ref, src_ref, d_attn_ref, in_width, total, (3, 4))
     raw_2_ref[...] = raw_ref[2 * rows :, :]
     tables = (gains_ref[...], cos_ref[...], sin_ref[...])
     attn_1, columns = back_attention(
@@ -286,7 +293,8 @@
 ):
     features = cot_ref.shape[1]
     in_width = raw_ref.shape[1]
-    rows_of(cot_ref, weights_ref, src_ref, d_attn_ref, in_width, weights_ref.shape[1])
+    d_attn_ref[...] = jnp.zeros(d_attn_ref.shape, F32)
+    rows_of(cot_ref, weights_ref, src_ref, d_attn_ref, in_width, weights_ref.shape[1], (0, SIDE))
     columns = back_attention(
         raw_ref[...], d_attn_ref[...].astype(BF16), gains_ref[...], cos_ref[...], sin_ref[...],
         terms_ref,
@@ -320,7 +328,8 @@
     in_width = raw_ref.shape[1]
     total = weights_ref.shape[1]
     normed_ref[...] = input_norm(x_ref[...], scale_ref[...])[2]
-    rows_of(normed_ref, weights_ref, src_ref, raw_ref, 0, in_width)
+    raw_ref[...] = jnp.zeros(raw_ref.shape, F32)
+    rows_of(normed_ref, weights_ref, src_ref, raw_ref, 0, in_width, (0, SIDE))
     attn = attend(raw_ref[...], gains_ref[...], cos_ref[...], sin_ref[...], total - in_width)[-1]
     columns_of(side_by_side(attn, rows), weights_ref, src_ref, part_ref, 0, in_width, total)
 
@@ -460,8 +469,14 @@
     whole = jax.ShapeDtypeStruct((features, total_width), BF16)
     gate = pieces[2][3]
     first_three = [held_until(piece, gate) for group in pieces[:2] for piece in group[3:]]
-    three = kernel_call(
-        three_groups_kernel, whole, info,
+    three, raw_3, d_attn_3 = kernel_call(
+        three_groups_kernel,
+        (
+            whole,
+            jax.ShapeDtypeStruct((3 * rows, in_width), F32),
+            jax.ShapeDtypeStruct((rows, q_width), F32),
+        ),
+        info, normed, cot_first,
         *pieces[0][:3], *first_three[:2], *pieces[1][:3], first_three[2], *pieces[2],
     )
     parts, early_block, terms_1, raw_2, weights = kernel_call(
@@ -473,8 +488,8 @@
             jax.ShapeDtypeStruct((rows, in_width), F32),
             whole,
         ),
-        info, normed, cot_first, *tables, *pieces[3], three,
-        aliases={10: 4},
+        info, normed, cot_first, *tables, raw_3, d_attn_3, *pieces[3], three,
+        aliases={12: 4},
         scratch=[pltpu.VMEM((3 * rows, in_width), F32), pltpu.VMEM((rows, q_width), F32)],
     )
     block = jax.ShapeDtypeStruct((rows, features), BF16)

time: 205 us -> 203 us (level)
  waiting for transfers between devices: 107 us -> 104 us
  transfers between devices with their start and end apart: 48 -> 48, of which waited for: 19 -> 19; matrix products, arithmetic and copies ran while one was open for 2% -> 2% of each run, Pallas kernels for 6% -> 7%
where the time goes in v1:
time: 203 us; the launch traced here: 200 us
  waiting for transfers between devices  104 us (51%)
  starting transfers between devices  66.5 us (33%)
  Pallas kernels  23.4 us (12%)
  other arithmetic  3.56 us (2%)
    ppermute x41, waiting for transfers between devices, along_dp(): return lax.ppermute(array, 'dp', route)  87.7 us
    ppermute x41, starting transfers between devices, along_dp(): return lax.ppermute(array, 'dp', route)  41.9 us
    pallas_call x8, Pallas kernels, kernel_call(): pl.pallas_call(kernel, in_specs=spec, out_specs=jax.tree.map(lambda _: pl...  23.4 us
    ppermute x5, starting transfers between devices, other_core(): return lax.ppermute(array, 'tensor', [(0, 1), (1, 0)])  14.8 us
    ppermute x1, waiting for transfers between devices, local(): passed = lax.ppermute(passed, ('section', 'tensor'), onward + back)  14.3 us
    ppermute x1, starting transfers between devices, local(): lax.ppermute(jnp.where(core == 0, stash[0, 0], stash[0, 1]), 'section', m...  8.53 us
  transfers between devices with their start and end apart: 48, of which 19 were waited for; matrix products, arithmetic and copies ran while one was open for 2% of the time, Pallas kernels for 7%

profile of v1, /device:TPU:1, one launch (start us, length us, event | category | flops | bytes accessed | tf_op | source)
XLA Modules:
  0.0 200.2 jit_solution(14136690400367701449)
XLA Ops:
  1.8 2.5 %collective-permute-start.5 = (bf16[128,2304]{1,0:T(8,128)(2,1)S(1)}, bf16[128,2304]{1,0:T(8,128)(2,1)S(1)}, u32[]{:S(2)}, u32[]{:S(2)}) collective-permute-start(bf16[128,2304]{1,0:T(8,128)(2,1)S(1)} %pad_maximum_fusion.refs_0_), channel_id=1, source_target_pairs={{0,8},{2,10},{4,12},{6,14},{8,24},{10,26},{12,28},{14,30},{16,0},{... | collective-permute-start | bytes 1769480 | tf_op jit(solution)/shard_map/ppermute | solution.py:39
  4.3 13.0 %collective-permute-done.5.refs_5_ = bf16[128,2304]{1,0:T(8,128)(2,1)S(1)} collective-permute-done((bf16[128,2304]{1,0:T(8,128)(2,1)S(1)}, bf16[128,2304]{1,0:T(8,128)(2,1)S(1)}, u32[]{:S(2)}, u32[]{:S(2)}) %collective-permute-start.5) | collective-permute-done | bytes 589856 | tf_op jit(solution)/shard_map/ppermute | solution.py:39
  17.4 2.6 %collective-permute-start.6 = (bf16[128,2304]{1,0:T(8,128)(2,1)S(1)}, bf16[128,2304]{1,0:T(8,128)(2,1)S(1)}, u32[]{:S(2)}, u32[]{:S(2)}) collective-permute-start(bf16[128,2304]{1,0:T(8,128)(2,1)S(1)} %collective-permute-done.5.refs_5_), channel_id=1, source_target_pairs={{0,2},{2,0},{4,6},{6,4},{8,10},{10,8},{12,14},{14,12},{16,18},{18,... | collective-permute-start | bytes 1769480 | tf_op jit(solution)/shard_map/ppermute | solution.py:39
  19.9 8.5 %collective-permute-start = (bf16[32,2048]{1,0:T(8,128)(2,1)S(1)}, bf16[32,2048]{1,0:T(8,128)(2,1)S(1)}, u32[]{:S(2)}, u32[]{:S(2)}) collective-permute-start(bf16[32,2048]{1,0:T(8,128)(2,1)S(1)} %select_bitcast_fusion), channel_id=1, source_target_pairs={{0,224},{32,192},{64,160},{96,128},{128,96},{160,64},{192,32},{224... | collective-permute-start | bytes 393224 | tf_op jit(solution)/shard_map/ppermute | solution.py:450
  31.0 4.0 %collective-permute-start.1 = (bf16[32,2048]{1,0:T(8,128)(2,1)S(1)}, bf16[32,2048]{1,0:T(8,128)(2,1)S(1)}, u32[]{:S(2)}, u32[]{:S(2)}) collective-permute-start(bf16[32,2048]{1,0:T(8,128)(2,1)S(1)} %collective-permute-done), channel_id=1, source_target_pairs={{0,1},{1,0},{2,3},{3,2},{4,5},{5,4},{6,7},{7,6},{8,9},{9,8},{10,11... | collective-permute-start | bytes 393224 | tf_op jit(solution)/shard_map/ppermute | solution.py:43
  38.1 17.1 %collective-permute-done.8.refs_7_ = bf16[128,2304]{1,0:T(8,128)(2,1)S(1)} collective-permute-done((bf16[128,2304]{1,0:T(8,128)(2,1)S(1)}, bf16[128,2304]{1,0:T(8,128)(2,1)S(1)}, u32[]{:S(2)}, u32[]{:S(2)}) %collective-permute-start.8) | collective-permute-done | bytes 589856 | tf_op jit(solution)/shard_map/ppermute | solution.py:39
  55.4 6.1 %collective-permute-done.7 = bf16[64,2304]{1,0:T(8,128)(2,1)S(1)} collective-permute-done((bf16[64,2304]{1,0:T(8,128)(2,1)S(1)}, bf16[64,2304]{1,0:T(8,128)(2,1)S(1)}, u32[]{:S(2)}, u32[]{:S(2)}) %collective-permute-start.7) | collective-permute-done | bytes 294944 | tf_op jit(solution)/shard_map/ppermute | solution.py:39
  62.8 3.1 %collective-permute-start.24 = (bf16[32,1536]{1,0:T(8,128)(2,1)S(1)}, bf16[32,1536]{1,0:T(8,128)(2,1)S(1)}, u32[]{:S(2)}, u32[]{:S(2)}) collective-permute-start(bf16[32,1536]{1,0:T(8,128)(2,1)S(1)} %get-tuple-element.63), channel_id=1, source_target_pairs={{0,4},{2,6},{4,0},{6,2},{8,12},{10,14},{12,8},{14,10},{16,20},{18,... | collective-permute-start | bytes 294920 | tf_op jit(solution)/shard_map/ppermute | solution.py:39
  71.3 4.2 %collective-permute-done.25 = bf16[32,1536]{1,0:T(8,128)(2,1)S(1)} collective-permute-done((bf16[32,1536]{1,0:T(8,128)(2,1)S(1)}, bf16[32,1536]{1,0:T(8,128)(2,1)S(1)}, u32[]{:S(2)}, u32[]{:S(2)}) %collective-permute-start.25) | collective-permute-done | bytes 98336 | tf_op jit(solution)/shard_map/ppermute | solution.py:39
  75.5 2.9 %collective-permute-start.14 = (bf16[128,2304]{1,0:T(8,128)(2,1)S(1)}, bf16[128,2304]{1,0:T(8,128)(2,1)S(1)}, u32[]{:S(2)}, u32[]{:S(2)}) collective-permute-start(bf16[128,2304]{1,0:T(8,128)(2,1)S(1)} %collective-permute-done.12.refs_9_), channel_id=1, source_target_pairs={{0,6},{2,4},{4,2},{6,0},{8,14},{10,12},{12,10},{14,8},{16,22},{18,... | collective-permute-start | bytes 1769480 | tf_op jit(solution)/shard_map/ppermute | solution.py:39
  80.0 9.5 %collective-permute-done.14.refs_11_ = bf16[128,2304]{1,0:T(8,128)(2,1)S(1)} collective-permute-done((bf16[128,2304]{1,0:T(8,128)(2,1)S(1)}, bf16[128,2304]{1,0:T(8,128)(2,1)S(1)}, u32[]{:S(2)}, u32[]{:S(2)}) %collective-permute-start.14) | collective-permute-done | bytes 589856 | tf_op jit(solution)/shard_map/ppermute | solution.py:39
  89.6 3.3 %shard_map.171 = (bf16[2048,2304]{1,0:T(8,128)(2,1)S(1)}, f32[96,1280]{1,0:T(8,128)S(1)}, f32[32,1024]{1,0:T(8,128)S(1)}) custom-call(s32[7]{0:T(128)S(1)} %concatenate.36.info_ref.src_ref.core_ref, bf16[96,2048]{1,0:T(8,128)(2,1)S(1)} %get-tuple-element.47.normed_ref, bf16[32,2048]{1,0:T(8,128)(2,1)S(1)} %bitcast.41, ...), custom_call_target="tpu_custom_call" | custom-call | tf_op jit(solution)/shard_map/pallas_call | solution.py:391
  92.9 7.2 %collective-permute-done.17.s2 = bf16[128,2304]{1,0:T(8,128)(2,1)S(1)} collective-permute-done((bf16[128,2304]{1,0:T(8,128)(2,1)S(1)}, bf16[128,2304]{1,0:T(8,128)(2,1)S(1)}, u32[]{:S(2)}, u32[]{:S(2)}) %collective-permute-start.17) | collective-permute-done | bytes 589856 | tf_op jit(solution)/shard_map/ppermute | solution.py:39
  100.2 5.8 %shard_map.172 = (bf16[64,2048]{1,0:T(8,128)(2,1)S(1)}, bf16[32,3328]{1,0:T(8,128)(2,1)S(1)}, f32[2,128]{1,0:T(2,128)S(1)}, f32[32,1280]{1,0:T(8,128)S(1)}, bf16[2048,2304]{1,0:T(8,128)(2,1)S(1)}) custom-call(s32[7]{0:T(128)S(1)} %concatenate.36.info_ref.src_ref.core_ref, ...), custom_call_target="tpu_custom_call", output_to_operand_aliasing={{4}: (12, {})} | custom-call | tf_op jit(solution)/shard_map/pallas_call | solution.py:391
  106.0 9.2 %collective-permute-start.19 = (bf16[64,2048]{1,0:T(8,128)(2,1)S(1)}, bf16[64,2048]{1,0:T(8,128)(2,1)S(1)}, u32[]{:S(2)}, u32[]{:S(2)}) collective-permute-start(bf16[64,2048]{1,0:T(8,128)(2,1)S(1)} %get-tuple-element.54.own_ref), channel_id=1, source_target_pairs={{0,1},{1,0},{2,3},{3,2},{4,5},{5,4},{6,7},{7,6},{8,9},{9,8},{10,11... | collective-permute-start | bytes 786440 | tf_op jit(solution)/shard_map/ppermute | solution.py:43
  121.1 14.3 %collective-permute-done.20 = bf16[32,2048]{1,0:T(8,128)(2,1)S(1)} collective-permute-done((bf16[32,2048]{1,0:T(8,128)(2,1)S(1)}, bf16[32,2048]{1,0:T(8,128)(2,1)S(1)}, u32[]{:S(2)}, u32[]{:S(2)}) %collective-permute-start.20) | collective-permute-done | bytes 131104 | tf_op jit(solution)/shard_map/ppermute | solution.py:505
  136.1 4.5 %collective-permute-done.30 = bf16[32,3328]{1,0:T(8,128)(2,1)S(1)} collective-permute-done((bf16[32,3328]{1,0:T(8,128)(2,1)S(1)}, bf16[32,3328]{1,0:T(8,128)(2,1)S(1)}, u32[]{:S(2)}, u32[]{:S(2)}) %collective-permute-start.30) | collective-permute-done | bytes 213024 | tf_op jit(solution)/shard_map/ppermute | solution.py:39
  140.6 4.2 %shard_map.174 = bf16[32,2048]{1,0:T(8,128)(2,1)S(1)} custom-call(s32[7]{0:T(128)S(1)} %concatenate.36.info_ref.src_ref.core_ref, bf16[32,2048]{1,0:T(8,128)(2,1)S(1)} %get-tuple-element.92.x_ref, f32[1,2048]{1,0:T(1,128)S(1)} %copy-done.2, f32[2,128]{1,0:T(2,128)S(1)} %bitcast.51, f32[256,128]{1,0:T(8,128)S(1)} %bitcast.35, f32[256,128]{1,0:T(8,128)S(1)} %bitcast.38, ...), custom_call_target="tpu_custom_call" | custom-call | tf_op jit(solution)/shard_map/pallas_call | solution.py:391
  144.8 4.5 %shard_map.175 = (bf16[32,1792]{1,0:T(8,128)(2,1)S(1)}, bf16[32,1792]{1,0:T(8,128)(2,1)S(1)}, bf16[32,1792]{1,0:T(8,128)(2,1)S(1)}, bf16[32,1792]{1,0:T(8,128)(2...) custom-call(s32[7]{0:T(128)S(1)} %concatenate.36.info_ref.src_ref.core_ref, ...), custom_call_target="tpu_custom_call" | custom-call | tf_op jit(solution)/shard_map/pallas_call | solution.py:391
  158.6 5.5 %collective-permute-done.38.c3 = bf16[32,1792]{1,0:T(8,128)(2,1)S(1)} collective-permute-done((bf16[32,1792]{1,0:T(8,128)(2,1)S(1)}, bf16[32,1792]{1,0:T(8,128)(2,1)S(1)}, u32[]{:S(2)}, u32[]{:S(2)}) %collective-permute-start.38) | collective-permute-done | bytes 114720 | tf_op jit(solution)/shard_map/ppermute | solution.py:39
  166.3 8.4 %collective-permute-done.45 = f32[18,128]{1,0:T(8,128)S(1)} collective-permute-done((f32[18,128]{1,0:T(8,128)S(1)}, f32[18,128]{1,0:T(8,128)S(1)}, u32[]{:S(2)}, u32[]{:S(2)}) %collective-permute-start.45) | collective-permute-done | bytes 9248 | tf_op jit(solution)/shard_map/ppermute | solution.py:39
  186.2 2.1 %collective-permute-start.41 = (bf16[64,1536]{1,0:T(8,128)(2,1)S(1)}, bf16[64,1536]{1,0:T(8,128)(2,1)S(1)}, u32[]{:S(2)}, u32[]{:S(2)}) collective-permute-start(bf16[64,1536]{1,0:T(8,128)(2,1)S(1)} %slice.161), channel_id=1, source_target_pairs={{0,6},{2,4},{4,2},{6,0},{8,14},{10,12},{12,10},{14,8},{16,22},{18,... | collective-permute-start | bytes 589832 | tf_op jit(solution)/shard_map/ppermute | solution.py:39
  190.4 6.6 %collective-permute-done.41.l3 = bf16[64,1536]{1,0:T(8,128)(2,1)S(1)} collective-permute-done((bf16[64,1536]{1,0:T(8,128)(2,1)S(1)}, bf16[64,1536]{1,0:T(8,128)(2,1)S(1)}, u32[]{:S(2)}, u32[]{:S(2)}) %collective-permute-start.41) | collective-permute-done | bytes 196640 | tf_op jit(solution)/shard_map/ppermute | solution.py:39
  197.0 3.2 %shard_map.177 = (f32[1,128,1024]{2,1,0:T(8,128)}, f32[1,128,128]{2,1,0:T(8,128)}, f32[1,128,128]{2,1,0:T(8,128)}, f32[1,128,1024]{2,1,0:T(8,128)}) custom-call(s32[7]{0:T(128)S(1)} %concatenate.36.info_ref.src_ref.core_ref, bf16[128,384]{1,0:T(8,128)(2,1)S(1)} %pad_maximum_fusion.2.n0, bf16[128,384]{1,0:T(8,128)(2,1)S(1)} %collective-permute-done.26.n1, ...), custom_call_target="tpu_custom_call" | custom-call | tf_op jit(solution)/shard_map/pallas_call | solution.py:391
  (146 shorter events, 46.7 us)
Async XLA Ops:
  1.8 15.6 %collective-permute-start.5 = (bf16[128,2304]{1,0:T(8,128)(2,1)S(1)}, bf16[128,2304]{1,0:T(8,128)(2,1)S(1)}, u32[]{:S(2)}, u32[]{:S(2)}) collective-permute-start(bf16[128,2304]{1,0:T(8,128)(2,1)S(1)} %pad_maximum_fusion.refs_0_), channel_id=1, source_target_pairs={{0,8},{2,10},{4,12},{6,14},{8,24},{10,26},{12,28},{14,30},{16,0},{... | collective-permute-start | bytes 1769480 | tf_op jit(solution)/shard_map/ppermute | solution.py:39
  17.4 19.5 %collective-permute-start.6 = (bf16[128,2304]{1,0:T(8,128)(2,1)S(1)}, bf16[128,2304]{1,0:T(8,128)(2,1)S(1)}, u32[]{:S(2)}, u32[]{:S(2)}) collective-permute-start(bf16[128,2304]{1,0:T(8,128)(2,1)S(1)} %collective-permute-done.5.refs_5_), channel_id=1, source_target_pairs={{0,2},{2,0},{4,6},{6,4},{8,10},{10,8},{12,14},{14,12},{16,18},{18,... | collective-permute-start | bytes 1769480 | tf_op jit(solution)/shard_map/ppermute | solution.py:39
  28.5 34.3 %collective-permute-start.3 = (bf16[128,2304]{1,0:T(8,128)(2,1)S(1)}, bf16[128,2304]{1,0:T(8,128)(2,1)S(1)}, u32[]{:S(2)}, u32[]{:S(2)}) collective-permute-start(bf16[128,2304]{1,0:T(8,128)(2,1)S(1)} %pad_maximum_fusion.refs_0_), channel_id=1, source_target_pairs={{0,6},{2,4},{4,2},{6,0},{8,14},{10,12},{12,10},{14,8},{16,22},{18,... | collective-permute-start | bytes 1769480 | tf_op jit(solution)/shard_map/ppermute | solution.py:39
  35.0 20.3 %collective-permute-start.12 = (bf16[128,2304]{1,0:T(8,128)(2,1)S(1)}, bf16[128,2304]{1,0:T(8,128)(2,1)S(1)}, u32[]{:S(2)}, u32[]{:S(2)}) collective-permute-start(bf16[128,2304]{1,0:T(8,128)(2,1)S(1)} %collective-permute-done.5.refs_5_), channel_id=1, source_target_pairs={{0,8},{2,10},{4,12},{6,14},{8,24},{10,26},{12,28},{14,30},{16,0},{... | collective-permute-start | bytes 1769480 | tf_op jit(solution)/shard_map/ppermute | solution.py:39
  35.0 20.2 %collective-permute-start.8 = (bf16[128,2304]{1,0:T(8,128)(2,1)S(1)}, bf16[128,2304]{1,0:T(8,128)(2,1)S(1)}, u32[]{:S(2)}, u32[]{:S(2)}) collective-permute-start(bf16[128,2304]{1,0:T(8,128)(2,1)S(1)} %collective-permute-done.5.refs_5_), channel_id=1, source_target_pairs={{0,6},{2,4},{4,2},{6,0},{8,14},{10,12},{12,10},{14,8},{16,22},{18,... | collective-permute-start | bytes 1769480 | tf_op jit(solution)/shard_map/ppermute | solution.py:39
  36.9 29.0 %collective-permute-start.2 = (bf16[128,2304]{1,0:T(8,128)(2,1)S(1)}, bf16[128,2304]{1,0:T(8,128)(2,1)S(1)}, u32[]{:S(2)}, u32[]{:S(2)}) collective-permute-start(bf16[128,2304]{1,0:T(8,128)(2,1)S(1)} %pad_maximum_fusion.refs_0_), channel_id=1, source_target_pairs={{0,2},{2,0},{4,6},{6,4},{8,10},{10,8},{12,14},{14,12},{16,18},{18,... | collective-permute-start | bytes 1769480 | tf_op jit(solution)/shard_map/ppermute | solution.py:39
  37.3 24.1 %collective-permute-start.7 = (bf16[64,2304]{1,0:T(8,128)(2,1)S(1)}, bf16[64,2304]{1,0:T(8,128)(2,1)S(1)}, u32[]{:S(2)}, u32[]{:S(2)}) collective-permute-start(bf16[64,2304]{1,0:T(8,128)(2,1)S(1)} %slice.139), channel_id=1, source_target_pairs={{0,6},{2,4},{4,2},{6,0},{8,14},{10,12},{12,10},{14,8},{16,22},{18,... | collective-permute-start | bytes 884744 | tf_op jit(solution)/shard_map/ppermute | solution.py:39
  55.3 23.1 %collective-permute-start.15 = (bf16[128,2304]{1,0:T(8,128)(2,1)S(1)}, bf16[128,2304]{1,0:T(8,128)(2,1)S(1)}, u32[]{:S(2)}, u32[]{:S(2)}) collective-permute-start(bf16[128,2304]{1,0:T(8,128)(2,1)S(1)} %collective-permute-done.12.refs_9_), channel_id=1, source_target_pairs={{0,8},{2,10},{4,12},{6,14},{8,24},{10,26},{12,28},{14,30},{16,0},{... | collective-permute-start | bytes 1769480 | tf_op jit(solution)/shard_map/ppermute | solution.py:39
  61.5 18.4 %collective-permute-start.10 = (bf16[128,2304]{1,0:T(8,128)(2,1)S(1)}, bf16[128,2304]{1,0:T(8,128)(2,1)S(1)}, u32[]{:S(2)}, u32[]{:S(2)}) collective-permute-start(bf16[128,2304]{1,0:T(8,128)(2,1)S(1)} %constant_dynamic-update-slice_fusion.refs_8_), channel_id=1, source_target_pairs={{0,8},{2,10},{4,12},{6,14},{8,24},{10,26},{12,28},{14,30},{16,0},{... | collective-permute-start | bytes 1769480 | tf_op jit(solution)/shard_map/ppermute | solution.py:39
  65.9 12.5 %collective-permute-start.11 = (bf16[64,2304]{1,0:T(8,128)(2,1)S(1)}, bf16[64,2304]{1,0:T(8,128)(2,1)S(1)}, u32[]{:S(2)}, u32[]{:S(2)}) collective-permute-start(bf16[64,2304]{1,0:T(8,128)(2,1)S(1)} %slice.142), channel_id=1, source_target_pairs={{0,2},{2,0},{4,6},{6,4},{8,10},{10,8},{12,14},{14,12},{16,18},{18,... | collective-permute-start | bytes 884744 | tf_op jit(solution)/shard_map/ppermute | solution.py:39
  75.5 14.1 %collective-permute-start.14 = (bf16[128,2304]{1,0:T(8,128)(2,1)S(1)}, bf16[128,2304]{1,0:T(8,128)(2,1)S(1)}, u32[]{:S(2)}, u32[]{:S(2)}) collective-permute-start(bf16[128,2304]{1,0:T(8,128)(2,1)S(1)} %collective-permute-done.12.refs_9_), channel_id=1, source_target_pairs={{0,6},{2,4},{4,2},{6,0},{8,14},{10,12},{12,10},{14,8},{16,22},{18,... | collective-permute-start | bytes 1769480 | tf_op jit(solution)/shard_map/ppermute | solution.py:39
  78.4 21.7 %collective-permute-start.17 = (bf16[128,2304]{1,0:T(8,128)(2,1)S(1)}, bf16[128,2304]{1,0:T(8,128)(2,1)S(1)}, u32[]{:S(2)}, u32[]{:S(2)}) collective-permute-start(bf16[128,2304]{1,0:T(8,128)(2,1)S(1)} %collective-permute-done.15.s0), channel_id=1, source_target_pairs={{0,6},{2,4},{4,2},{6,0},{8,14},{10,12},{12,10},{14,8},{16,22},{18,... | collective-permute-start | bytes 1769480 | tf_op jit(solution)/shard_map/ppermute | solution.py:39
  78.5 21.6 %collective-permute-start.16 = (bf16[128,2304]{1,0:T(8,128)(2,1)S(1)}, bf16[128,2304]{1,0:T(8,128)(2,1)S(1)}, u32[]{:S(2)}, u32[]{:S(2)}) collective-permute-start(bf16[128,2304]{1,0:T(8,128)(2,1)S(1)} %collective-permute-done.15.s0), channel_id=1, source_target_pairs={{0,2},{2,0},{4,6},{6,4},{8,10},{10,8},{12,14},{14,12},{16,18},{18,... | collective-permute-start | bytes 1769480 | tf_op jit(solution)/shard_map/ppermute | solution.py:39
  79.9 20.2 %collective-permute-start.18 = (bf16[128,2304]{1,0:T(8,128)(2,1)S(1)}, bf16[128,2304]{1,0:T(8,128)(2,1)S(1)}, u32[]{:S(2)}, u32[]{:S(2)}) collective-permute-start(bf16[128,2304]{1,0:T(8,128)(2,1)S(1)} %collective-permute-done.10.refs_12_), channel_id=1, source_target_pairs={{0,8},{2,10},{4,12},{6,14},{8,24},{10,26},{12,28},{14,30},{16,0},{... | collective-permute-start | bytes 1769480 | tf_op jit(solution)/shard_map/ppermute | solution.py:39
  106.0 12.9 %collective-permute-start.19 = (bf16[64,2048]{1,0:T(8,128)(2,1)S(1)}, bf16[64,2048]{1,0:T(8,128)(2,1)S(1)}, u32[]{:S(2)}, u32[]{:S(2)}) collective-permute-start(bf16[64,2048]{1,0:T(8,128)(2,1)S(1)} %get-tuple-element.54.own_ref), channel_id=1, source_target_pairs={{0,1},{1,0},{2,3},{3,2},{4,5},{5,4},{6,7},{7,6},{8,9},{9,8},{10,11... | collective-permute-start | bytes 786440 | tf_op jit(solution)/shard_map/ppermute | solution.py:43
  115.3 35.2 %collective-permute-start.31 = (bf16[32,3328]{1,0:T(8,128)(2,1)S(1)}, bf16[32,3328]{1,0:T(8,128)(2,1)S(1)}, u32[]{:S(2)}, u32[]{:S(2)}) collective-permute-start(bf16[32,3328]{1,0:T(8,128)(2,1)S(1)} %get-tuple-element.65), channel_id=1, source_target_pairs={{0,24},{2,26},{4,28},{6,30},{8,16},{10,18},{12,20},{14,22},{16,8},... | collective-permute-start | bytes 638984 | tf_op jit(solution)/shard_map/ppermute | solution.py:39
  117.0 23.6 %collective-permute-start.30 = (bf16[32,3328]{1,0:T(8,128)(2,1)S(1)}, bf16[32,3328]{1,0:T(8,128)(2,1)S(1)}, u32[]{:S(2)}, u32[]{:S(2)}) collective-permute-start(bf16[32,3328]{1,0:T(8,128)(2,1)S(1)} %get-tuple-element.65), channel_id=1, source_target_pairs={{0,16},{2,18},{4,20},{6,22},{8,24},{10,26},{12,28},{14,30},{16,0},... | collective-permute-start | bytes 638984 | tf_op jit(solution)/shard_map/ppermute | solution.py:39
  117.4 18.7 %collective-permute-start.29 = (bf16[32,3328]{1,0:T(8,128)(2,1)S(1)}, bf16[32,3328]{1,0:T(8,128)(2,1)S(1)}, u32[]{:S(2)}, u32[]{:S(2)}) collective-permute-start(bf16[32,3328]{1,0:T(8,128)(2,1)S(1)} %get-tuple-element.65), channel_id=1, source_target_pairs={{0,8},{2,10},{4,12},{6,14},{8,0},{10,2},{12,4},{14,6},{16,24},{18,... | collective-permute-start | bytes 638984 | tf_op jit(solution)/shard_map/ppermute | solution.py:39
  119.8 15.7 %collective-permute-start.20 = (bf16[32,2048]{1,0:T(8,128)(2,1)S(1)}, bf16[32,2048]{1,0:T(8,128)(2,1)S(1)}, u32[]{:S(2)}, u32[]{:S(2)}) collective-permute-start(bf16[32,2048]{1,0:T(8,128)(2,1)S(1)} %get-tuple-element.56), channel_id=1, source_target_pairs={{0,32},{32,64},{64,96},{96,128},{128,160},{160,192},{192,224},{33,... | collective-permute-start | bytes 393224 | tf_op jit(solution)/shard_map/ppermute | solution.py:505
  152.3 27.2 %collective-permute-start.33 = (bf16[128,3328]{1,0:T(8,128)(2,1)S(1)}, bf16[128,3328]{1,0:T(8,128)(2,1)S(1)}, u32[]{:S(2)}, u32[]{:S(2)}) collective-permute-start(bf16[128,3328]{1,0:T(8,128)(2,1)S(1)} %constant_dynamic-update-slice_fusion.2.e0), channel_id=1, source_target_pairs={{0,6},{2,4},{4,2},{6,0},{8,14},{10,12},{12,10},{14,8},{16,22},{18,... | collective-permute-start | bytes 2555912 | tf_op jit(solution)/shard_map/ppermute | solution.py:39
  154.2 26.0 %collective-permute-start.32 = (bf16[128,3328]{1,0:T(8,128)(2,1)S(1)}, bf16[128,3328]{1,0:T(8,128)(2,1)S(1)}, u32[]{:S(2)}, u32[]{:S(2)}) collective-permute-start(bf16[128,3328]{1,0:T(8,128)(2,1)S(1)} %constant_dynamic-update-slice_fusion.2.e0), channel_id=1, source_target_pairs={{0,2},{2,0},{4,6},{6,4},{8,10},{10,8},{12,14},{14,12},{16,18},{18,... | collective-permute-start | bytes 2555912 | tf_op jit(solution)/shard_map/ppermute | solution.py:39
  166.1 16.9 %collective-permute-start.39 = (bf16[128,1536]{1,0:T(8,128)(2,1)S(1)}, bf16[128,1536]{1,0:T(8,128)(2,1)S(1)}, u32[]{:S(2)}, u32[]{:S(2)}) collective-permute-start(bf16[128,1536]{1,0:T(8,128)(2,1)S(1)} %get-tuple-element.77), channel_id=1, source_target_pairs={{0,2},{2,0},{4,6},{6,4},{8,10},{10,8},{12,14},{14,12},{16,18},{18,... | collective-permute-start | bytes 1179656 | tf_op jit(solution)/shard_map/ppermute | solution.py:39
  181.7 15.3 %collective-permute-start.35 = (bf16[64,3328]{1,0:T(8,128)(2,1)S(1)}, bf16[64,3328]{1,0:T(8,128)(2,1)S(1)}, u32[]{:S(2)}, u32[]{:S(2)}) collective-permute-start(bf16[64,3328]{1,0:T(8,128)(2,1)S(1)} %slice.159), channel_id=1, source_target_pairs={{0,2},{2,0},{4,6},{6,4},{8,10},{10,8},{12,14},{14,12},{16,18},{18,... | collective-permute-start | bytes 1277960 | tf_op jit(solution)/shard_map/ppermute | solution.py:39
  183.0 14.0 %collective-permute-start.34 = (bf16[64,3328]{1,0:T(8,128)(2,1)S(1)}, bf16[64,3328]{1,0:T(8,128)(2,1)S(1)}, u32[]{:S(2)}, u32[]{:S(2)}) collective-permute-start(bf16[64,3328]{1,0:T(8,128)(2,1)S(1)} %slice.158), channel_id=1, source_target_pairs={{0,6},{2,4},{4,2},{6,0},{8,14},{10,12},{12,10},{14,8},{16,22},{18,... | collective-permute-start | bytes 1277960 | tf_op jit(solution)/shard_map/ppermute | solution.py:39
  (31 other events, 331.9 us)
